TPU v7x, 32 devices: a whole 2x2x4 slice. The times are simulated.
32 devices in a mesh: dp: 8 (over z, x), mp: 4 (over y, core).
Axes of the slice: x: 2, y: 2, z: 4, core: 2. Of those that a mesh axis runs over, the one named last changes fastest.
Arguments:
- tokens: bfloat16 [32768, 1024], P('dp'), may hold values from -12 to 12
- out_grad: bfloat16 [32768, 1024], P('dp'), may hold values from -12 to 12
- qk_weight: float32 [2, 1024, 256], P(None, 'dp'), may hold values from -0.1875 to 0.1875
- qk_first: float32 [2, 1024, 256], P(None, 'dp'), may hold values from -0.0048828125 to 0.0048828125
- qk_second: float32 [2, 1024, 256], P(None, 'dp'), may hold values from 5.839972e-07 to 2.3359887e-06
- qk_average: float32 [2, 1024, 256], P(None, 'dp'), may hold values from -0.1875 to 0.1875
- value_weight: float32 [1024, 1024], P('dp', 'mp'), may hold values from -0.1875 to 0.1875
- value_first: float32 [1024, 1024], P('dp', 'mp'), may hold values from -0.0024414062 to 0.0024414062
- value_second: float32 [1024, 1024], P('dp', 'mp'), may hold values from 1.9069296e-07 to 7.6277183e-07
- value_average: float32 [1024, 1024], P('dp', 'mp'), may hold values from -0.1875 to 0.1875
- output_weight: float32 [1024, 1024], P('mp', 'dp'), may hold values from -1.5 to 1.5
- output_first: float32 [1024, 1024], P('mp', 'dp'), may hold values from -0.00048828125 to 0.00048828125
- output_second: float32 [1024, 1024], P('mp', 'dp'), may hold values from 6.7040493e-09 to 2.6816197e-08
- output_average: float32 [1024, 1024], P('mp', 'dp'), may hold values from -1.5 to 1.5
- gate_up_weight: float32 [2, 1024, 2752], P(None, 'dp', 'mp'), may hold values from -0.1875 to 0.1875
- gate_up_first: float32 [2, 1024, 2752], P(None, 'dp', 'mp'), may hold values from -0.0009765625 to 0.0009765625
- gate_up_second: float32 [2, 1024, 2752], P(None, 'dp', 'mp'), may hold values from 3.2775354e-08 to 1.3110142e-07
- gate_up_average: float32 [2, 1024, 2752], P(None, 'dp', 'mp'), may hold values from -0.1875 to 0.1875
- down_weight: float32 [2752, 1024], P('mp', 'dp'), may hold values from -0.109375 to 0.109375
- down_first: float32 [2752, 1024], P('mp', 'dp'), may hold values from -0.001953125 to 0.001953125
- down_second: float32 [2752, 1024], P('mp', 'dp'), may hold values from 1.0726479e-07 to 4.2905916e-07
- down_average: float32 [2752, 1024], P('mp', 'dp'), may hold values from -0.109375 to 0.109375
- gains: float32 [2, 1024], P(None, 'dp'), may hold values from 0.5 to 1.5
- gains_first: float32 [2, 1024], P(None, 'dp'), may hold values from -0.0034179688 to 0.0034179688
- gains_second: float32 [2, 1024], P(None, 'dp'), may hold values from 2.9795777e-07 to 1.1918311e-06
- gains_average: float32 [2, 1024], P(None, 'dp'), may hold values from 0.5 to 1.5
Outputs:
- block_out: bfloat16 [32768, 1024], P('dp', 'mp')
- input_grad: float32 [32768, 1024], P('dp', 'mp')
- grad_norm: float32 [], replicated
- qk_first_new: float32 [2, 1024, 256], P(None, 'dp')
- qk_second_new: float32 [2, 1024, 256], P(None, 'dp')
- qk_new: float32 [2, 1024, 256], P(None, 'dp')
- qk_average_new: float32 [2, 1024, 256], P(None, 'dp')
- value_first_new: float32 [1024, 1024], P('dp', 'mp')
- value_second_new: float32 [1024, 1024], P('dp', 'mp')
- value_new: float32 [1024, 1024], P('dp', 'mp')
- value_average_new: float32 [1024, 1024], P('dp', 'mp')
- output_first_new: float32 [1024, 1024], P('mp', 'dp')
- output_second_new: float32 [1024, 1024], P('mp', 'dp')
- output_new: float32 [1024, 1024], P('mp', 'dp')
- output_average_new: float32 [1024, 1024], P('mp', 'dp')
- gate_up_first_new: float32 [2, 1024, 2752], P(None, 'dp', 'mp')
- gate_up_second_new: float32 [2, 1024, 2752], P(None, 'dp', 'mp')
- gate_up_new: float32 [2, 1024, 2752], P(None, 'dp', 'mp')
- gate_up_average_new: float32 [2, 1024, 2752], P(None, 'dp', 'mp')
- down_first_new: float32 [2752, 1024], P('mp', 'dp')
- down_second_new: float32 [2752, 1024], P('mp', 'dp')
- down_new: float32 [2752, 1024], P('mp', 'dp')
- down_average_new: float32 [2752, 1024], P('mp', 'dp')
- gains_first_new: float32 [2, 1024], P(None, 'dp')
- gains_second_new: float32 [2, 1024], P(None, 'dp')
- gains_new: float32 [2, 1024], P(None, 'dp')
- gains_average_new: float32 [2, 1024], P(None, 'dp')
All inputs are finite; a program needn't handle non-finite values.
Results may differ from a plain program's by a relative error of at most 0.018.
Values may be sent and summed in bfloat16 or wider, within the bound.
A program may use at most 256 MiB of HBM per device.

v0:
```python
import math
import jax
import jax.numpy as jnp
from jax import lax
from jax.sharding import PartitionSpec as P

D = 1024
H = 16
F = 16
VH = 64
FF = 2752
V_ALL = 1024
LEN = 1024
STEP = 5


def inner(left, right):
    return lax.dot_general(
        left, right, (((0,), (0,)), ((), ())), preferred_element_type=jnp.float32
    )


def against(left, right):
    return lax.dot_general(
        left, right, (((1,), (1,)), ((), ())), preferred_element_type=jnp.float32
    )


def rms_scale(values):
    return lax.rsqrt(jnp.mean(values * values, axis=1, keepdims=True) + 1e-05)


def score_table(query, keys):
    length = query.shape[0]
    causal = (jnp.arange(length)[:, None] >= jnp.arange(length)[None, :]).astype(jnp.float32)
    tiled = jnp.einsum("ihf,jhf->hij", query, keys, preferred_element_type=jnp.float32) / math.sqrt(
        query.shape[2]
    )
    return (tiled, causal)


def mix_forward(parts):
    query, keys, values = parts
    tiled, causal = score_table(query, keys)
    kernel = causal * (1.0 + tiled + 0.5 * tiled * tiled)
    numer = jnp.einsum(
        "hij,jhv->ihv", kernel.astype(jnp.bfloat16), values, preferred_element_type=jnp.float32
    )
    return (numer, jnp.sum(kernel, axis=2).T)


def mix_backward(parts):
    query, keys, values, numer, denom, grad_mixed = parts
    tiled, causal = score_table(query, keys)
    kernel = causal * (1.0 + tiled + 0.5 * tiled * tiled)
    grad_numer = (grad_mixed / denom[:, :, None]).astype(jnp.bfloat16)
    grad_denom = -jnp.sum(grad_mixed * numer, axis=2) / (denom * denom)
    grad_kernel = (
        jnp.einsum("ihv,jhv->hij", grad_numer, values, preferred_element_type=jnp.float32)
        + grad_denom.T[:, :, None]
    )
    grad_tiled = (causal * grad_kernel * (1.0 + tiled)).astype(jnp.bfloat16)
    root = math.sqrt(query.shape[2])
    grad_values = jnp.einsum(
        "hij,ihv->jhv", kernel.astype(jnp.bfloat16), grad_numer, preferred_element_type=jnp.float32
    ).astype(jnp.bfloat16)
    grad_query = (
        jnp.einsum("hij,jhf->ihf", grad_tiled, keys, preferred_element_type=jnp.float32) / root
    ).astype(jnp.bfloat16)
    grad_keys = (
        jnp.einsum("hij,ihf->jhf", grad_tiled, query, preferred_element_type=jnp.float32) / root
    ).astype(jnp.bfloat16)
    return (grad_query, grad_keys, grad_values)


def adam_step(grad, first, second, weight, average, rate):
    first = 0.5 * first + 0.5 * grad
    second = 0.5 * second + 0.5 * grad * grad
    correct = 1.0 - 0.5**STEP
    weight = weight - rate * (first / correct / (jnp.sqrt(second / correct) + 1e-08) + 0.1 * weight)
    average = 0.5 * average + 0.5 * weight
    return (first, second, weight, average)


def on_device(
    tokens,
    out_grad,
    qk_weight,
    qk_first,
    qk_second,
    qk_average,
    value_weight,
    value_first,
    value_second,
    value_average,
    output_weight,
    output_first,
    output_second,
    output_average,
    gate_up_weight,
    gate_up_first,
    gate_up_second,
    gate_up_average,
    down_weight,
    down_first,
    down_second,
    down_average,
    gains,
    gains_first,
    gains_second,
    gains_average,
):
    groups = lax.axis_size("mp")
    rank = lax.axis_index("mp")
    qk_full, value_local, output_local, gate_up_local, down_local, gains_full = (
        lax.all_gather(qk_weight.astype(jnp.bfloat16), "dp", axis=1, tiled=True),
        lax.all_gather(value_weight.astype(jnp.bfloat16), "dp", axis=0, tiled=True),
        lax.all_gather(output_weight.astype(jnp.bfloat16), "dp", axis=1, tiled=True),
        lax.all_gather(gate_up_weight.astype(jnp.bfloat16), "dp", axis=1, tiled=True),
        lax.all_gather(down_weight.astype(jnp.bfloat16), "dp", axis=1, tiled=True),
        lax.all_gather(gains.astype(jnp.bfloat16), "dp", axis=1, tiled=True),
    )
    width = qk_full.shape[2] // groups
    qk_local = lax.dynamic_slice_in_dim(qk_full, rank * width, width, 2)
    tok_count = tokens.shape[0]
    seq_count = tok_count // LEN
    heads_here = H // groups
    cols = tokens.shape[1] // groups
    col_start = rank * cols
    first_gain = gains_full[0].astype(jnp.float32)
    second_gain = gains_full[1].astype(jnp.float32)
    inputs = tokens.astype(jnp.float32)
    scale_one = rms_scale(inputs)
    normed_one = inputs * scale_one
    hidden_one = (normed_one * first_gain).astype(jnp.bfloat16)
    query = jnp.dot(hidden_one, qk_local[0], preferred_element_type=jnp.float32).astype(
        jnp.bfloat16
    )
    keys = jnp.dot(hidden_one, qk_local[1], preferred_element_type=jnp.float32).astype(jnp.bfloat16)
    values = jnp.dot(hidden_one, value_local, preferred_element_type=jnp.float32).astype(
        jnp.bfloat16
    )
    head_query = query.reshape(seq_count, LEN, heads_here, F)
    head_keys = keys.reshape(seq_count, LEN, heads_here, F)
    head_values = values.reshape(seq_count, LEN, heads_here, VH)
    numer, denom = lax.map(mix_forward, (head_query, head_keys, head_values))
    mixed = (numer / denom[:, :, :, None]).astype(jnp.bfloat16).reshape(tok_count, heads_here * VH)
    attn_part = jnp.dot(mixed, output_local, preferred_element_type=jnp.float32)
    resid = inputs + lax.psum(attn_part.astype(jnp.bfloat16), "mp").astype(jnp.float32)
    scale_two = rms_scale(resid)
    normed_two = resid * scale_two
    hidden_two = (normed_two * second_gain).astype(jnp.bfloat16)
    gate = jnp.dot(hidden_two, gate_up_local[0], preferred_element_type=jnp.float32)
    lift = jnp.dot(hidden_two, gate_up_local[1], preferred_element_type=jnp.float32)
    sigma = jax.nn.sigmoid(gate)
    activ = (gate * sigma * lift).astype(jnp.bfloat16)
    down_part = jnp.dot(activ, down_local, preferred_element_type=jnp.float32)
    block_out = (
        lax.dynamic_slice_in_dim(resid, col_start, cols, 1)
        + lax.psum_scatter(
            down_part.astype(jnp.bfloat16), "mp", scatter_dimension=1, tiled=True
        ).astype(jnp.float32)
    ).astype(jnp.bfloat16)
    cotan = out_grad.astype(jnp.float32)
    grad_activ = against(out_grad, down_local)
    down_grad = inner(activ, out_grad)
    grad_gate = (grad_activ * lift * sigma * (1.0 + gate * (1.0 - sigma))).astype(jnp.bfloat16)
    grad_lift = (grad_activ * gate * sigma).astype(jnp.bfloat16)
    gate_up_grad = jnp.stack((inner(hidden_two, grad_gate), inner(hidden_two, grad_lift)))
    back_two = lax.psum(
        (against(grad_gate, gate_up_local[0]) + against(grad_lift, gate_up_local[1])).astype(
            jnp.bfloat16
        ),
        "mp",
    ).astype(jnp.float32)
    gain_two = jnp.sum(back_two * normed_two, axis=0)
    grad_resid = (
        cotan
        + scale_two * second_gain * back_two
        - resid * scale_two**3 * jnp.mean(resid * second_gain * back_two, axis=1, keepdims=True)
    )
    resid_low = grad_resid.astype(jnp.bfloat16)
    output_grad = inner(mixed, resid_low)
    grad_mixed = against(resid_low, output_local).reshape(seq_count, LEN, heads_here, VH)
    grad_query, grad_keys, grad_values = lax.map(
        mix_backward, (head_query, head_keys, head_values, numer, denom, grad_mixed)
    )
    grad_query = grad_query.reshape(tok_count, width)
    grad_keys = grad_keys.reshape(tok_count, width)
    grad_values = grad_values.reshape(tok_count, heads_here * VH)
    qk_grad = jnp.stack((inner(hidden_one, grad_query), inner(hidden_one, grad_keys)))
    value_grad = inner(hidden_one, grad_values)
    back_one = (
        against(grad_query, qk_local[0])
        + against(grad_keys, qk_local[1])
        + against(grad_values, value_local)
    )
    input_part = scale_one * first_gain * back_one - inputs * scale_one**3 * jnp.mean(
        inputs * first_gain * back_one, axis=1, keepdims=True
    )
    gains_grad = jnp.stack((jnp.sum(back_one * normed_one, axis=0), gain_two))
    input_grad = lax.dynamic_slice_in_dim(grad_resid, col_start, cols, 1) + lax.psum_scatter(
        input_part.astype(jnp.bfloat16), "mp", scatter_dimension=1, tiled=True
    ).astype(jnp.float32)
    qk_grad = lax.all_gather(qk_grad.astype(jnp.bfloat16), "mp", axis=2, tiled=True).astype(
        qk_grad.dtype
    )
    qk_share, value_share, output_share, gate_up_share, down_share, gains_share = (
        lax.psum_scatter(qk_grad, "dp", scatter_dimension=1, tiled=True),
        lax.psum_scatter(value_grad, "dp", scatter_dimension=0, tiled=True),
        lax.psum_scatter(output_grad, "dp", scatter_dimension=1, tiled=True),
        lax.psum_scatter(gate_up_grad, "dp", scatter_dimension=1, tiled=True),
        lax.psum_scatter(down_grad, "dp", scatter_dimension=1, tiled=True),
        lax.psum_scatter(gains_grad, "dp", scatter_dimension=1, tiled=True),
    )
    first_row = lax.psum(gains_share[0], "mp")
    gains_share = jnp.stack((first_row, gains_share[1]))
    spread_sum = (
        jnp.sum(value_share * value_share)
        + jnp.sum(output_share * output_share)
        + jnp.sum(gate_up_share * gate_up_share)
        + jnp.sum(down_share * down_share)
    )
    shared_sum = jnp.sum(qk_share * qk_share) + jnp.sum(gains_share * gains_share)
    total = lax.psum(spread_sum + shared_sum / groups, ("dp", "mp"))
    grad_norm = jnp.sqrt(total)
    clip = jnp.minimum(1.0, 1.0 / (grad_norm + 1e-06))
    qk_m, qk_v, qk_w, qk_a = adam_step(
        clip * qk_share, qk_first, qk_second, qk_weight, qk_average, 1.0 / math.sqrt(D)
    )
    value_m, value_v, value_w, value_a = adam_step(
        clip * value_share,
        value_first,
        value_second,
        value_weight,
        value_average,
        1.0 / math.sqrt(D),
    )
    output_m, output_v, output_w, output_a = adam_step(
        clip * output_share,
        output_first,
        output_second,
        output_weight,
        output_average,
        1.0 / math.sqrt(max(1, V_ALL * 16 // LEN)),
    )
    gate_up_m, gate_up_v, gate_up_w, gate_up_a = adam_step(
        clip * gate_up_share,
        gate_up_first,
        gate_up_second,
        gate_up_weight,
        gate_up_average,
        1.0 / math.sqrt(D),
    )
    down_m, down_v, down_w, down_a = adam_step(
        clip * down_share, down_first, down_second, down_weight, down_average, 1.0 / math.sqrt(FF)
    )
    gains_m, gains_v, gains_w, gains_a = adam_step(
        clip * gains_share, gains_first, gains_second, gains, gains_average, 0.4
    )
    return (
        block_out,
        input_grad,
        grad_norm,
        qk_m,
        qk_v,
        qk_w,
        qk_a,
        value_m,
        value_v,
        value_w,
        value_a,
        output_m,
        output_v,
        output_w,
        output_a,
        gate_up_m,
        gate_up_v,
        gate_up_w,
        gate_up_a,
        down_m,
        down_v,
        down_w,
        down_a,
        gains_m,
        gains_v,
        gains_w,
        gains_a,
    )


def solution(mesh):
    placed = (
        P("dp", None),
        P("dp", None),
        P(None, "dp", None),
        P(None, "dp", None),
        P(None, "dp", None),
        P(None, "dp", None),
        P("dp", "mp"),
        P("dp", "mp"),
        P("dp", "mp"),
        P("dp", "mp"),
        P("mp", "dp"),
        P("mp", "dp"),
        P("mp", "dp"),
        P("mp", "dp"),
        P(None, "dp", "mp"),
        P(None, "dp", "mp"),
        P(None, "dp", "mp"),
        P(None, "dp", "mp"),
        P("mp", "dp"),
        P("mp", "dp"),
        P("mp", "dp"),
        P("mp", "dp"),
        P(None, "dp"),
        P(None, "dp"),
        P(None, "dp"),
        P(None, "dp"),
    )
    return jax.shard_map(
        on_device,
        mesh=mesh,
        in_specs=placed,
        out_specs=(
            P("dp", "mp"),
            P("dp", "mp"),
            P(),
            P(None, "dp", None),
            P(None, "dp", None),
            P(None, "dp", None),
            P(None, "dp", None),
            P("dp", "mp"),
            P("dp", "mp"),
            P("dp", "mp"),
            P("dp", "mp"),
            P("mp", "dp"),
            P("mp", "dp"),
            P("mp", "dp"),
            P("mp", "dp"),
            P(None, "dp", "mp"),
            P(None, "dp", "mp"),
            P(None, "dp", "mp"),
            P(None, "dp", "mp"),
            P("mp", "dp"),
            P("mp", "dp"),
            P("mp", "dp"),
            P("mp", "dp"),
            P(None, "dp"),
            P(None, "dp"),
            P(None, "dp"),
            P(None, "dp"),
        ),
        check_vma=False,
    )
```

profile of v0, /device:TPU:0, one launch (start us, length us, event | category | flops | bytes accessed | tf_op | source)
XLA Modules:
  0.0 1489.0 jit_solution(11503148982517520819)
XLA Ops:
  9.9 22.2 %all_gather.21 = bf16[2,1024]{1,0:T(2,128)(2,1)S(1)} all-gather(bf16[2,128]{1,0:T(2,128)(2,1)S(1)} %convert_element_type.163), channel_id=1, replica_groups=mesh['dp'=8,'mp'=4] {'dp'}, dimensions={1}, use_global_device_ids=true | all-gather | bytes 4608 | tf_op jit(solution)/shard_map/all_gather | solution.py:121
  32.2 5.1 fusion.56
  37.9 31.9 %all_gather.22 = bf16[1024,256]{1,0:T(8,128)(2,1)S(1)} all-gather(bf16[128,256]{1,0:T(8,128)(2,1)S(1)} %convert_element_type.165), channel_id=1, replica_groups=mesh['dp'=8,'mp'=4] {'dp'}, dimensions={0}, use_global_device_ids=true | all-gather | bytes 589824 | tf_op jit(solution)/shard_map/all_gather | solution.py:117
  80.9 5.6 copy.95
  86.5 28.1 %all_gather.24 = bf16[256,1024]{1,0:T(8,128)(2,1)} all-gather(bf16[256,128]{1,0:T(8,128)(2,1)S(1)} %convert_element_type.171), channel_id=1, replica_groups=mesh['dp'=8,'mp'=4] {'dp'}, dimensions={1}, use_global_device_ids=true | all-gather | bytes 589824 | tf_op jit(solution)/shard_map/all_gather | solution.py:118
  114.6 6.1 convolution_convert_fusion.3
  121.3 6.1 convolution_convert_fusion.4
  129.8 35.0 %while.30 = (s32[]{:T(128)}, f32[4,1024,4,64]{1,3,2,0:T(8,128)}, f32[4,1024,4]{1,2,0:T(4,128)S(1)}, bf16[4,1024,4,64]{1,3,2,0:T(8,128)(2,1)S(1)}, bf16[4,1024,4,...) while((s32[]{:T(128)}, f32[4,1024,4,64]{1,3,2,0:T(8,128)}, ...), condition=%wide.region_3.4_spmd, body=%wide.region_1.3_spmd.sunk | while | flops 706736128 | bytes 27052120 | solution.py:146
  130.5 5.6 fusion.150
  139.2 5.6 fusion.150
  147.9 5.6 fusion.150
  156.6 5.6 fusion.150
  164.8 4.0 divide_convert_fusion.3
  172.6 5.7 convolution_convert_fusion.1
  181.0 148.5 %all-reduce.3.cloned.1.call-done = bf16[4096,1024]{1,0:T(8,128)(2,1)} async-done(((bf16[4096,1024]{1,0:T(8,128)(2,1)}), bf16[4096,1024]{1,0:T(8,128)(2,1)}) %all-reduce.3.cloned.1.call-update) | async-done | bytes 8388624 | tf_op jit(solution)/shard_map/psum | solution.py:149
  329.6 8.6 multiply_reduce_fusion
  338.1 10.8 multiply_convert_fusion.9
  348.9 42.7 %all-gather.7.cloned.1.call-done = bf16[2,1024,688]{1,2,0:T(8,128)(2,1)} async-done(((bf16[2,128,688]{1,2,0:T(8,128)(2,1)}), bf16[2,1024,688]{1,2,0:T(8,128)(2,1)}) %all-gather.7.cloned.1.call-update) | async-done | bytes 2818064 | tf_op jit(solution)/shard_map/all_gather | solution.py:119
  391.6 12.5 fusion.68
  404.1 8.8 fusion.67
  412.9 22.6 %all-gather.9.cloned.1.call-done = bf16[688,1024]{1,0:T(8,128)(2,1)} async-done(((bf16[688,128]{1,0:T(8,128)(2,1)}), bf16[688,1024]{1,0:T(8,128)(2,1)}) %all-gather.9.cloned.1.call-update) | async-done | bytes 1409040 | tf_op jit(solution)/shard_map/all_gather | solution.py:120
  435.5 22.1 %multiply_convert_fusion.10 = (bf16[4096,688]{0,1:T(8,128)(2,1)}, bf16[4096,688]{0,1:T(8,128)(2,1)}, bf16[4096,688]{0,1:T(8,128)(2,1)}) fusion(f32[4096,688]{0,1:T(8,128)} %fusion.67, f32[4096,688]{0,1:T(8,128)} %fusion.68, bf16[4096,1024]{1,0:T(8,128)(2,1)} %param.31, bf16[688,1024]{1,0:T(8,128)(2,1)} %all-gather.9.cloned.1.call-done), kind=kOutput, calls=%fused_computation.84 | convolution fusion | flops 5816451072 | bytes 49250304 | tf_op jit(solution)/shard_map/dot_general | solution.py:24
  457.6 13.2 fusion.66
  470.8 12.5 add_convert_fusion
  483.4 151.4 %all-reduce.5.cloned.1.call-done = bf16[4096,1024]{1,0:T(8,128)(2,1)} async-done(((bf16[4096,1024]{1,0:T(8,128)(2,1)}), bf16[4096,1024]{1,0:T(8,128)(2,1)}) %all-reduce.5.cloned.1.call-update) | async-done | bytes 8388624 | tf_op jit(solution)/shard_map/psum | solution.py:170
  634.8 12.0 fusion.55
  646.8 17.5 %fusion.53 = (f32[4096,1024]{1,0:T(8,128)S(1)}, f32[4096,1024]{1,0:T(8,128)}) fusion(bf16[4096,1024]{1,0:T(8,128)(2,1)} %all-reduce.5.cloned.1.call-done, bf16[4096,1024]{1,0:T(8,128)(2,1)} %param.31, f32[4096]{0:T(1024)S(1)} %broadcast_multiply_fusion.1, f32[4096]{0:T(1024)S(1)} %get-tuple-element.439, f32[1024]{0:T(1024)S(1)} %bitcast.225, ...), kind=kLoop, calls=%fused_computation.71 | loop fusion | flops 46137344 | bytes 67162112 | tf_op jit(solution)/shard_map/sub | solution.py:178
  664.3 5.7 copy-done.5
  670.1 4.4 fusion.64
  674.4 6.0 reshape.148
  680.5 141.2 %while.31 = (s32[]{:T(128)}, bf16[4,1024,4,16]{1,3,2,0:T(8,128)(2,1)}, bf16[4,1024,4,16]{1,3,2,0:T(8,128)(2,1)}, bf16[4,1024,4,64]{1,3,2,0:T(8,128)(2,1)}, bf16[...) while((s32[]{:T(128)}, ...), condition=%wide.region_11.12_spmd, body=%wide.region_9.11_spmd.sunk | while | flops 1535123456 | bytes 167644336 | solution.py:185
  690.7 5.7 copy-done
  696.4 4.8 fusion.165
  701.1 8.3 multiply_convert_fusion.16
  725.8 5.7 copy-done
  731.5 4.7 fusion.165
  736.3 8.3 multiply_convert_fusion.16
  761.0 5.7 copy-done
  766.7 4.7 fusion.165
  771.4 8.3 multiply_convert_fusion.16
  796.2 5.7 copy-done
  801.9 4.7 fusion.165
  806.6 8.3 multiply_convert_fusion.16
  832.6 9.6 fusion.75
  842.3 9.3 fusion.74
  851.6 18.5 %fusion.51 = (f32[1024]{0:T(1024)S(1)}, f32[4096]{0:T(1024)S(1)}, f32[4096,1024]{1,0:T(8,128)}) fusion(bf16[4096,1024]{1,0:T(8,128)(2,1)S(1)} %bitcast.205, f32[4096]{0:T(1024)S(1)} %copy-done.29, f32[1024]{0:T(1024)S(1)} %bitcast.221, bf16[4096,256]{0,1:T(8,128)(2,1)S(1)} %bitcast.208, bf16[1024,256]{1,0:T(8,128)(2,1)} %copy-done.19, ...), kind=kOutput, calls=%fused_computation.69 | convolution fusion | flops 2185227264 | bytes 61382656 | tf_op jit(solution)/shard_map/dot_general | solution.py:24
  871.2 11.6 fusion.92
  882.9 9.2 fusion.62
  892.1 7.4 fusion.91
  902.5 10.3 convolution_bitcast_fusion
  912.8 10.1 convolution_bitcast_fusion.1
  926.0 11.8 convolution_convert_fusion
  938.5 12.5 fusion.59
  953.7 6.1 psum.30
  960.4 50.7 %reduce-scatter.21.cloned.1.call-done = f32[688,128]{1,0:T(8,128)} async-done(((f32[688,1024]{1,0:T(8,128)}), f32[688,128]{1,0:T(8,128)}) %reduce-scatter.21.cloned.1.call-update) | async-done | bytes 352272 | tf_op jit(solution)/shard_map/reduce_scatter | solution.py:213
  1012.9 64.5 %reduce-scatter.17.cloned.1.call-done = f32[256,128]{1,0:T(8,128)} async-done(((f32[256,1024]{1,0:T(8,128)}), f32[256,128]{1,0:T(8,128)}) %reduce-scatter.17.cloned.1.call-update) | async-done | bytes 131088 | tf_op jit(solution)/shard_map/reduce_scatter | solution.py:211
  1078.9 64.1 %reduce-scatter.15.cloned.1.call-done = f32[128,256]{1,0:T(8,128)} async-done(((f32[1024,256]{1,0:T(8,128)}), f32[128,256]{1,0:T(8,128)}) %reduce-scatter.15.cloned.1.call-update) | async-done | bytes 131088 | tf_op jit(solution)/shard_map/reduce_scatter | solution.py:210
  1145.9 69.1 %reduce-scatter.23.cloned.1.call-done = f32[2,128,256]{1,2,0:T(8,128)} async-done(((f32[2,1024,256]{1,2,0:T(8,128)}), f32[2,128,256]{1,2,0:T(8,128)}) %reduce-scatter.23.cloned.1.call-update) | async-done | bytes 262160 | tf_op jit(solution)/shard_map/reduce_scatter | solution.py:209
  1217.9 108.5 %reduce-scatter.19.cloned.1.call-done = f32[2,128,688]{1,2,0:T(8,128)} async-done(((f32[2,1024,688]{1,2,0:T(8,128)}), f32[2,128,688]{1,2,0:T(8,128)}) %reduce-scatter.19.cloned.1.call-update) | async-done | bytes 704528 | tf_op jit(solution)/shard_map/reduce_scatter | solution.py:212
  1329.7 40.8 %psum.31 = f32[]{:T(128)} all-reduce(f32[]{:T(128)S(6)} %add.280), channel_id=1, replica_groups=mesh['dp'=8,'mp'=4] {'dp','mp'}, use_global_device_ids=true, to_apply=%region_29.30 | all-reduce | flops 1 | bytes 8 | tf_op jit(solution)/shard_map/psum | solution.py:225
  1390.8 10.6 reduce-scatter.11.cloned.1.call-done
  1401.4 4.6 add_convert_fusion.1
  1406.0 69.6 %reduce-scatter.13.cloned.1.call-done = bf16[4096,256]{1,0:T(8,128)(2,1)} async-done(((bf16[4096,1024]{1,0:T(8,128)(2,1)}), bf16[4096,256]{1,0:T(8,128)(2,1)}) %reduce-scatter.13.cloned.1.call-update) | async-done | bytes 2097168 | tf_op jit(solution)/shard_map/reduce_scatter | solution.py:202
  1475.6 5.2 convert_add_fusion.1
  (230 shorter events, 151.4 us)
Async XLA Ops:
  7.2 30.7 %copy-start.24 = (f32[128,256]{1,0:T(8,128)S(1)}, f32[128,256]{1,0:T(8,128)}, u32[]{:S(2)}) copy-start(f32[128,256]{1,0:T(8,128)} %param.36) | copy-start | bytes 393220
  7.2 30.7 %copy-start.26 = (f32[256,128]{1,0:T(8,128)S(1)}, f32[256,128]{1,0:T(8,128)}, u32[]{:S(2)}) copy-start(f32[256,128]{1,0:T(8,128)} %param.40) | copy-start | bytes 393220
  7.2 107.4 %all-gather.5.cloned.1.call-start = ((), (), s32[]{:S(2)}) async-start(), calls=%async_computation.8 | async-start | bytes 1179648 | tf_op jit(solution)/shard_map/all_gather | solution.py:116
  9.0 320.6 %all-reduce.3.cloned.1.call-start = ((), (), s32[]{:S(2)}) async-start(), calls=%async_computation.9 | async-start | bytes 16777216 | tf_op jit(solution)/shard_map/psum | solution.py:149
  9.0 60.8 %copy-start.1 = (bf16[4096,1024]{1,0:T(8,128)(2,1)S(1)}, bf16[4096,1024]{1,0:T(8,128)(2,1)}, u32[]{:S(2)}) copy-start(bf16[4096,1024]{1,0:T(8,128)(2,1)} %param.30) | copy-start | bytes 25165828
  32.2 40.0 %copy-start.34 = (f32[1,1024]{1,0:T(1,128)}, f32[1,1024]{1,0:T(1,128)S(1)}, u32[]{:S(2)}) copy-start(f32[1,1024]{1,0:T(1,128)S(1)} %get-tuple-element.441) | copy-start | bytes 12292
  37.9 32.0 %copy-start.28 = (f32[4096]{0:T(1024)}, f32[4096]{0:T(1024)S(1)}, u32[]{:S(2)}) copy-start(f32[4096]{0:T(1024)S(1)} %get-tuple-element.438) | copy-start | bytes 49156
  69.9 2.3 copy-start.19
  72.1 3.2 copy-start.2
  164.8 6.5 copy-start.30
  164.8 13.5 copy-start.6
  164.8 13.5 copy-start.12
  164.8 13.5 copy-start.13
  164.8 7.8 copy-start.14
  171.3 1.3 copy-start.7
  178.3 2.0 copy-start.20
  178.3 1.2 copy-start.16
  178.3 213.3 %all-gather.7.cloned.1.call-start = ((), (), s32[]{:S(2)}) async-start(), calls=%async_computation.10 | async-start | bytes 3170304 | tf_op jit(solution)/shard_map/all_gather | solution.py:119
  180.2 255.3 %all-gather.9.cloned.1.call-start = ((), (), s32[]{:S(2)}) async-start(), calls=%async_computation.11 | async-start | bytes 1585152 | tf_op jit(solution)/shard_map/all_gather | solution.py:120
  181.0 453.8 %all-reduce.5.cloned.1.call-start = ((), (), s32[]{:S(2)}) async-start(), calls=%async_computation.13 | async-start | bytes 16777216 | tf_op jit(solution)/shard_map/psum | solution.py:170
  391.6 12.5 copy-start.10
  391.6 12.5 copy-start.40
  457.6 13.2 copy-start.42
  483.3 416.3 %all-gather.11.cloned.1.call-start = ((), (), s32[]{:S(2)}) async-start(), calls=%async_computation.19 | async-start | bytes 1310720 | tf_op jit(solution)/shard_map/all_gather | solution.py:205
  646.8 23.2 %copy-start.15 = (bf16[256,1024]{1,0:T(8,128)(2,1)S(1)}, bf16[256,1024]{1,0:T(8,128)(2,1)}, u32[]{:S(2)}) copy-start(bf16[256,1024]{1,0:T(8,128)(2,1)} %all_gather.24) | copy-start | bytes 1572868
  664.3 5.7 copy-start.5
  684.1 6.5 copy-start.4
  690.6 5.7 copy-start
  719.3 6.5 copy-start.4
  725.8 5.7 copy-start
  754.5 6.5 copy-start.4
  761.0 5.7 copy-start
  789.6 6.5 copy-start.4
  796.2 5.7 copy-start
  821.7 6.3 copy-start.3
  825.9 25.6 %copy-start.9 = (bf16[32,8,4,1024]{3,1,2,0:T(8,128)(2,1)}, bf16[32,8,4,1024]{3,1,2,0:T(8,128)(2,1)S(1)}, u32[]{:S(2)}) copy-start(bf16[32,8,4,1024]{3,1,2,0:T(8,128)(2,1)S(1)} %copy.128) | copy-start | bytes 6291460
  828.0 1.6 copy-start.27
  830.2 1.6 copy-start.11
  832.6 120.0 %reduce-scatter.25.cloned.1.call-start = ((), (), s32[]{:S(2)}) async-start(), calls=%async_computation.21 | async-start | bytes 589824
  832.6 18.9 %slice-start = ((s8[8388608]{0:T(1024)(128)(4,1)}), s8[4194304]{0:T(1024)(128)(4,1)S(1)}, s32[]{:S(2)}) async-start(s8[8388608]{0:T(1024)(128)(4,1)} %bitcast.204), calls=%async_computation.22 | async-start | bytes 8388608
  842.3 9.3 slice-start.1
  842.3 9.3 copy-start.29
  842.3 9.3 copy-start.35
  851.6 18.5 %copy-start.37 = (f32[1024]{0:T(1024)S(1)}, f32[1024]{0:T(1024)}, u32[]{:S(2)}) copy-start(f32[1024]{0:T(1024)} %get-tuple-element.368) | copy-start | bytes 12292
  871.1 140.0 %reduce-scatter.21.cloned.1.call-start = ((), (), s32[]{:S(2)}) async-start(), calls=%async_computation.18 | async-start | bytes 3170304 | tf_op jit(solution)/shard_map/reduce_scatter | solution.py:213
  871.2 11.7 copy-start.8
  882.9 194.5 %reduce-scatter.17.cloned.1.call-start = ((), (), s32[]{:S(2)}) async-start(), calls=%async_computation.16 | async-start | bytes 1179648 | tf_op jit(solution)/shard_map/reduce_scatter | solution.py:211
  892.1 250.9 %reduce-scatter.15.cloned.1.call-start = ((), (), s32[]{:S(2)}) async-start(), calls=%async_computation.15 | async-start | bytes 1179648 | tf_op jit(solution)/shard_map/reduce_scatter | solution.py:210
  899.6 315.4 %reduce-scatter.23.cloned.1.call-start = ((), (), s32[]{:S(2)}) async-start(), calls=%async_computation.20 | async-start | bytes 2359296 | tf_op jit(solution)/shard_map/reduce_scatter | solution.py:209
  902.5 423.9 %reduce-scatter.19.cloned.1.call-start = ((), (), s32[]{:S(2)}) async-start(), calls=%async_computation.17 | async-start | bytes 6340608 | tf_op jit(solution)/shard_map/reduce_scatter | solution.py:212
  922.9 3.1 copy-start.41
  926.0 475.4 %reduce-scatter.11.cloned.1.call-start = ((), (), s32[]{:S(2)}) async-start(), calls=%async_computation.12 | async-start | bytes 10485760 | tf_op jit(solution)/shard_map/reduce_scatter | solution.py:160
  937.8 537.8 %reduce-scatter.13.cloned.1.call-start = ((), (), s32[]{:S(2)}) async-start(), calls=%async_computation.14 | async-start | bytes 10485760 | tf_op jit(solution)/shard_map/reduce_scatter | solution.py:202
  951.0 0.9 copy-start.23
  951.0 1.1 copy-start.31
  951.0 1.2 copy-start.32
  951.0 1.4 copy-start.33
  951.0 429.8 %copy-start.25 = (f32[128,256]{1,0:T(8,128)S(1)}, f32[128,256]{1,0:T(8,128)}, u32[]{:S(2)}) copy-start(f32[128,256]{1,0:T(8,128)} %param.36) | copy-start | bytes 393220
  951.1 433.7 %copy-start.21 = (f32[688,128]{1,0:T(8,128)S(1)}, f32[688,128]{1,0:T(8,128)}, u32[]{:S(2)}) copy-start(f32[688,128]{1,0:T(8,128)} %param.48) | copy-start | bytes 1056772
  951.1 436.2 %copy-start.17 = (f32[2,128,688]{1,2,0:T(8,128)S(1)}, f32[2,128,688]{1,2,0:T(8,128)}, u32[]{:S(2)}) copy-start(f32[2,128,688]{1,2,0:T(8,128)} %param.44) | copy-start | bytes 2113540
  953.7 417.5 %copy-start.38 = (f32[1,128]{1,0:T(1,128)}, f32[1,128]{1,0:T(1,128)S(1)}, u32[]{:S(2)}) copy-start(f32[1,128]{1,0:T(1,128)S(1)} %copy.124) | copy-start | bytes 1540
  959.8 411.4 %copy-start.39 = (f32[1,128]{1,0:T(1,128)}, f32[1,128]{1,0:T(1,128)S(1)}, u32[]{:S(2)}) copy-start(f32[1,128]{1,0:T(1,128)S(1)} %psum.30) | copy-start | bytes 1540
  1011.1 373.6 %copy-start.22 = (f32[688,128]{1,0:T(8,128)S(1)}, f32[688,128]{1,0:T(8,128)}, u32[]{:S(2)}) copy-start(f32[688,128]{1,0:T(8,128)} %reduce-scatter.21.cloned.1.call-done) | copy-start | bytes 1056772
  1326.4 60.9 %copy-start.18 = (f32[2,128,688]{1,2,0:T(8,128)S(1)}, f32[2,128,688]{1,2,0:T(8,128)}, u32[]{:S(2)}) copy-start(f32[2,128,688]{1,2,0:T(8,128)} %reduce-scatter.19.cloned.1.call-done) | copy-start | bytes 2113540
  (1 other events, 0.7 us)
Sparse Core Ops, SparseCore 0:
  10.8 46.0 all-gather.4
  178.4 151.0 all-reduce.2
  332.2 59.3 all-gather.6
  394.1 41.3 all-gather.8
  483.5 151.3 all-reduce.4
  832.7 16.8 all-gather.10
  871.3 62.0 reduce-scatter.24
  937.9 73.2 reduce-scatter.20
  1014.9 62.3 reduce-scatter.16
  1080.6 62.3 reduce-scatter.14
  1147.6 67.3 reduce-scatter.22
  1218.9 107.4 reduce-scatter.18
  1329.2 72.2 reduce-scatter.10
  1403.8 71.7 reduce-scatter.12
where the time goes:
time: 1500 us; the launch traced here: 1490 us
  waiting for transfers between devices  802 us (53%)
  matrix products  319 us (21%)
  other arithmetic  131 us (9%)
  blocking collectives  129 us (9%)
  local copies, waits for them, and re-layouts  84.8 us (6%)
  between operations  20.9 us (1%)
    psum x1, waiting for transfers between devices, on_device(): lax.psum((against(grad_gate, gate_up_local[0]) + against(grad_lift, gate_...  151 us
    psum x1, waiting for transfers between devices, on_device(): lax.psum(attn_part.astype(jnp.bfloat16), 'mp').astype(jnp.float32)  149 us
    reduce_scatter x1, waiting for transfers between devices, on_device(): lax.psum_scatter(gate_up_grad, 'dp', scatter_dimension=1, tiled=True)  108 us
    dot_general x7, matrix products, against(): lax.dot_general(left, right, (((1,), (1,)), ((), ())), preferred_element_...  89.6 us
    reduce_scatter x1, waiting for transfers between devices, on_device(): lax.psum_scatter(input_part.astype(jnp.bfloat16), 'mp', scatter_dimension...  69.6 us
    reduce_scatter x1, waiting for transfers between devices, on_device(): lax.psum_scatter(qk_grad, 'dp', scatter_dimension=1, tiled=True)  69.1 us
    reduce_scatter x1, waiting for transfers between devices, on_device(): lax.psum_scatter(output_grad, 'dp', scatter_dimension=1, tiled=True)  64.5 us
    reduce_scatter x1, waiting for transfers between devices, on_device(): lax.psum_scatter(value_grad, 'dp', scatter_dimension=0, tiled=True)  64.1 us
  transfers between devices with their start and end apart: 14, of which 11 were waited for; matrix products, arithmetic and copies ran while one was open for 14% of the time, Pallas kernels for 0%

commit v1 on v0

--- a/solution.py
+++ b/solution.py
@@ -146,7 +146,9 @@
     numer, denom = lax.map(mix_forward, (head_query, head_keys, head_values))
     mixed = (numer / denom[:, :, :, None]).astype(jnp.bfloat16).reshape(tok_count, heads_here * VH)
     attn_part = jnp.dot(mixed, output_local, preferred_element_type=jnp.float32)
-    resid = inputs + lax.psum(attn_part.astype(jnp.bfloat16), "mp").astype(jnp.float32)
+    resid = inputs + jnp.sum(lax.all_gather(attn_part.astype(jnp.bfloat16), "mp"), axis=0).astype(
+        jnp.float32
+    )
     scale_two = rms_scale(resid)
     normed_two = resid * scale_two
     hidden_two = (normed_two * second_gain).astype(jnp.bfloat16)

time: 1500 us -> 1550 us (1.033)
  waiting for transfers between devices: 802 us -> 833 us
  other arithmetic: 131 us -> 147 us
    all_gather x0 -> x1, waiting for transfers between devices: none -> 197 us  [on_device(): lax.all_gather(attn_part.astype(jnp.bfloat16), 'mp')]
    psum x1 -> x0, waiting for transfers between devices: 149 us -> none  [on_device(): lax.psum(attn_part.astype(jnp.bfloat16), 'mp').astype(jnp.float32)]
    reduce_sum x0 -> x1, other arithmetic: none -> 17.2 us  [on_device(): jnp.sum(lax.all_gather(attn_part.astype(jnp.bfloat16), 'mp'), axis=0)]
    all_gather x1, waiting for transfers between devices: 42.7 us -> 25.9 us  [on_device(): lax.all_gather(gate_up_weight.astype(jnp.bfloat16), 'dp', axis=1, tiled=T...]
  transfers between devices with their start and end apart: 14 -> 14, of which waited for: 11 -> 11; matrix products, arithmetic and copies ran while one was open for 14% -> 15% of each run, Pallas kernels for 0% -> 0%
where the time goes in v1:
time: 1550 us; the launch traced here: 1540 us
  waiting for transfers between devices  833 us (54%)
  matrix products  319 us (21%)
  other arithmetic  147 us (9%)
  blocking collectives  129 us (8%)
  local copies, waits for them, and re-layouts  84.8 us (5%)
  between operations  20.9 us (1%)
    all_gather x1, waiting for transfers between devices, on_device(): lax.all_gather(attn_part.astype(jnp.bfloat16), 'mp')  197 us
    psum x1, waiting for transfers between devices, on_device(): lax.psum((against(grad_gate, gate_up_local[0]) + against(grad_lift, gate_...  151 us
    reduce_scatter x1, waiting for transfers between devices, on_device(): lax.psum_scatter(gate_up_grad, 'dp', scatter_dimension=1, tiled=True)  109 us
    dot_general x7, matrix products, against(): lax.dot_general(left, right, (((1,), (1,)), ((), ())), preferred_element_...  89.7 us
    reduce_scatter x1, waiting for transfers between devices, on_device(): lax.psum_scatter(input_part.astype(jnp.bfloat16), 'mp', scatter_dimension...  69.6 us
    reduce_scatter x1, waiting for transfers between devices, on_device(): lax.psum_scatter(qk_grad, 'dp', scatter_dimension=1, tiled=True)  68.8 us
    reduce_scatter x1, waiting for transfers between devices, on_device(): lax.psum_scatter(output_grad, 'dp', scatter_dimension=1, tiled=True)  64.5 us
    reduce_scatter x1, waiting for transfers between devices, on_device(): lax.psum_scatter(value_grad, 'dp', scatter_dimension=0, tiled=True)  64 us
  transfers between devices with their start and end apart: 14, of which 11 were waited for; matrix products, arithmetic and copies ran while one was open for 15% of the time, Pallas kernels for 0%

profile of v1, /device:TPU:0, one launch (start us, length us, event | category | flops | bytes accessed | tf_op | source)
XLA Modules:
  0.0 1536.3 jit_solution(3107563501415771057)
XLA Ops:
  9.9 22.2 %all_gather.27 = bf16[2,1024]{1,0:T(2,128)(2,1)S(1)} all-gather(bf16[2,128]{1,0:T(2,128)(2,1)S(1)} %convert_element_type.165), channel_id=1, replica_groups=mesh['dp'=8,'mp'=4] {'dp'}, dimensions={1}, use_global_device_ids=true | all-gather | bytes 4608 | tf_op jit(solution)/shard_map/all_gather | solution.py:121
  32.2 5.1 fusion.56
  37.9 31.9 %all_gather.28 = bf16[1024,256]{1,0:T(8,128)(2,1)S(1)} all-gather(bf16[128,256]{1,0:T(8,128)(2,1)S(1)} %convert_element_type.167), channel_id=1, replica_groups=mesh['dp'=8,'mp'=4] {'dp'}, dimensions={0}, use_global_device_ids=true | all-gather | bytes 589824 | tf_op jit(solution)/shard_map/all_gather | solution.py:117
  80.9 5.6 copy.95
  86.5 28.1 %all_gather.30 = bf16[256,1024]{1,0:T(8,128)(2,1)} all-gather(bf16[256,128]{1,0:T(8,128)(2,1)S(1)} %convert_element_type.173), channel_id=1, replica_groups=mesh['dp'=8,'mp'=4] {'dp'}, dimensions={1}, use_global_device_ids=true | all-gather | bytes 589824 | tf_op jit(solution)/shard_map/all_gather | solution.py:118
  114.6 6.1 convolution_convert_fusion.3
  121.3 6.1 convolution_convert_fusion.4
  129.8 35.0 %while.30 = (s32[]{:T(128)}, f32[4,1024,4,64]{1,3,2,0:T(8,128)}, f32[4,1024,4]{1,2,0:T(4,128)S(1)}, bf16[4,1024,4,64]{1,3,2,0:T(8,128)(2,1)S(1)}, bf16[4,1024,4,...) while((s32[]{:T(128)}, f32[4,1024,4,64]{1,3,2,0:T(8,128)}, ...), condition=%wide.region_3.4_spmd, body=%wide.region_1.3_spmd.sunk | while | flops 706736128 | bytes 27052120 | solution.py:146
  130.5 5.6 fusion.150
  139.2 5.6 fusion.150
  147.9 5.6 fusion.150
  156.6 5.6 fusion.150
  172.6 5.6 convolution_convert_fusion.1
  181.0 197.0 %all-gather.15.cloned.1.call-done = bf16[16384,1024]{1,0:T(8,128)(2,1)} async-done(((bf16[4096,1024]{1,0:T(8,128)(2,1)}), bf16[16384,1024]{1,0:T(8,128)(2,1)}) %all-gather.15.cloned.1.call-update) | async-done | bytes 33554448 | tf_op jit(solution)/shard_map/all_gather | solution.py:149
  378.1 17.2 %reduce_sum.145 = bf16[4096,1024]{1,0:T(8,128)(2,1)} reduce(bf16[4,4096,1024]{2,1,0:T(8,128)(2,1)} %bitcast.207, bf16[]{:T(256)} %constant.172.clone.1), dimensions={0}, to_apply=%region_4.5 | reduce | flops 12582912 | bytes 41943040 | tf_op jit(solution)/shard_map/reduce_sum | solution.py:149
  395.3 8.6 multiply_reduce_fusion
  403.9 10.1 multiply_convert_fusion.9
  414.0 25.9 %all-gather.9.cloned.1.call-done = bf16[2,1024,688]{1,2,0:T(8,128)(2,1)} async-done(((bf16[2,128,688]{1,2,0:T(8,128)(2,1)}), bf16[2,1024,688]{1,2,0:T(8,128)(2,1)}) %all-gather.9.cloned.1.call-update) | async-done | bytes 2818064 | tf_op jit(solution)/shard_map/all_gather | solution.py:119
  439.9 12.5 fusion.68
  452.4 8.8 fusion.67
  461.3 22.5 %all-gather.11.cloned.1.call-done = bf16[688,1024]{1,0:T(8,128)(2,1)} async-done(((bf16[688,128]{1,0:T(8,128)(2,1)}), bf16[688,1024]{1,0:T(8,128)(2,1)}) %all-gather.11.cloned.1.call-update) | async-done | bytes 1409040 | tf_op jit(solution)/shard_map/all_gather | solution.py:120
  483.8 22.3 %multiply_convert_fusion.10 = (bf16[4096,688]{0,1:T(8,128)(2,1)}, bf16[4096,688]{0,1:T(8,128)(2,1)}, bf16[4096,688]{0,1:T(8,128)(2,1)}) fusion(f32[4096,688]{0,1:T(8,128)} %fusion.67, f32[4096,688]{0,1:T(8,128)} %fusion.68, bf16[4096,1024]{1,0:T(8,128)(2,1)} %param.31, bf16[688,1024]{1,0:T(8,128)(2,1)} %all-gather.11.cloned.1.call-done), kind=kOutput, calls=%fused_computation.84 | convolution fusion | flops 5816451072 | bytes 49250304 | tf_op jit(solution)/shard_map/dot_general | solution.py:24
  506.1 13.0 fusion.66
  519.2 12.5 add_convert_fusion
  531.8 151.4 %all-reduce.2.cloned.1.call-done = bf16[4096,1024]{1,0:T(8,128)(2,1)} async-done(((bf16[4096,1024]{1,0:T(8,128)(2,1)}), bf16[4096,1024]{1,0:T(8,128)(2,1)}) %all-reduce.2.cloned.1.call-update) | async-done | bytes 8388624 | tf_op jit(solution)/shard_map/psum | solution.py:172
  683.2 12.0 fusion.55
  695.2 17.5 %fusion.53 = (f32[4096,1024]{1,0:T(8,128)S(1)}, f32[4096,1024]{1,0:T(8,128)}) fusion(bf16[4096,1024]{1,0:T(8,128)(2,1)} %all-reduce.2.cloned.1.call-done, bf16[4096,1024]{1,0:T(8,128)(2,1)} %param.31, f32[4096]{0:T(1024)S(1)} %broadcast_multiply_fusion.1, f32[4096]{0:T(1024)S(1)} %get-tuple-element.439, f32[1024]{0:T(1024)S(1)} %bitcast.227, ...), kind=kLoop, calls=%fused_computation.71 | loop fusion | flops 46137344 | bytes 67162112 | tf_op jit(solution)/shard_map/sub | solution.py:180
  712.7 5.7 copy-done.5
  718.5 4.4 fusion.64
  722.8 6.0 reshape.148
  728.9 141.2 %while.31 = (s32[]{:T(128)}, bf16[4,1024,4,16]{1,3,2,0:T(8,128)(2,1)}, bf16[4,1024,4,16]{1,3,2,0:T(8,128)(2,1)}, bf16[4,1024,4,64]{1,3,2,0:T(8,128)(2,1)}, bf16[...) while((s32[]{:T(128)}, ...), condition=%wide.region_11.12_spmd, body=%wide.region_9.11_spmd.sunk | while | flops 1535123456 | bytes 167644336 | solution.py:187
  739.1 5.7 copy-done
  744.8 4.8 fusion.165
  749.5 8.3 multiply_convert_fusion.16
  774.2 5.7 copy-done
  779.9 4.7 fusion.165
  784.7 8.3 multiply_convert_fusion.16
  809.4 5.7 copy-done
  815.1 4.7 fusion.165
  819.9 8.3 multiply_convert_fusion.16
  844.6 5.7 copy-done
  850.3 4.7 fusion.165
  855.0 8.3 multiply_convert_fusion.16
  881.0 9.6 fusion.75
  890.7 9.3 fusion.74
  900.0 18.5 %fusion.51 = (f32[1024]{0:T(1024)S(1)}, f32[4096]{0:T(1024)S(1)}, f32[4096,1024]{1,0:T(8,128)}) fusion(bf16[4096,1024]{1,0:T(8,128)(2,1)S(1)} %bitcast.206, f32[4096]{0:T(1024)S(1)} %copy-done.29, f32[1024]{0:T(1024)S(1)} %bitcast.223, bf16[4096,256]{0,1:T(8,128)(2,1)S(1)} %bitcast.210, bf16[1024,256]{1,0:T(8,128)(2,1)} %copy-done.19, ...), kind=kOutput, calls=%fused_computation.69 | convolution fusion | flops 2185227264 | bytes 61382656 | tf_op jit(solution)/shard_map/dot_general | solution.py:24
  919.6 11.6 fusion.92
  931.3 9.2 fusion.62
  940.6 7.4 fusion.91
  950.9 10.3 convolution_bitcast_fusion
  961.2 10.1 convolution_bitcast_fusion.1
  974.4 11.8 convolution_convert_fusion
  986.9 12.5 fusion.59
  1002.1 6.1 psum.22
  1008.8 49.8 %reduce-scatter.21.cloned.1.call-done = f32[688,128]{1,0:T(8,128)} async-done(((f32[688,1024]{1,0:T(8,128)}), f32[688,128]{1,0:T(8,128)}) %reduce-scatter.21.cloned.1.call-update) | async-done | bytes 352272 | tf_op jit(solution)/shard_map/reduce_scatter | solution.py:215
  1060.4 64.5 %reduce-scatter.17.cloned.1.call-done = f32[256,128]{1,0:T(8,128)} async-done(((f32[256,1024]{1,0:T(8,128)}), f32[256,128]{1,0:T(8,128)}) %reduce-scatter.17.cloned.1.call-update) | async-done | bytes 131088 | tf_op jit(solution)/shard_map/reduce_scatter | solution.py:213
  1126.4 64.0 %reduce-scatter.15.cloned.1.call-done = f32[128,256]{1,0:T(8,128)} async-done(((f32[1024,256]{1,0:T(8,128)}), f32[128,256]{1,0:T(8,128)}) %reduce-scatter.15.cloned.1.call-update) | async-done | bytes 131088 | tf_op jit(solution)/shard_map/reduce_scatter | solution.py:212
  1193.3 68.8 %reduce-scatter.23.cloned.1.call-done = f32[2,128,256]{1,2,0:T(8,128)} async-done(((f32[2,1024,256]{1,2,0:T(8,128)}), f32[2,128,256]{1,2,0:T(8,128)}) %reduce-scatter.23.cloned.1.call-update) | async-done | bytes 262160 | tf_op jit(solution)/shard_map/reduce_scatter | solution.py:211
  1265.1 108.6 %reduce-scatter.19.cloned.1.call-done = f32[2,128,688]{1,2,0:T(8,128)} async-done(((f32[2,1024,688]{1,2,0:T(8,128)}), f32[2,128,688]{1,2,0:T(8,128)}) %reduce-scatter.19.cloned.1.call-update) | async-done | bytes 704528 | tf_op jit(solution)/shard_map/reduce_scatter | solution.py:214
  1377.0 40.7 %psum.23 = f32[]{:T(128)} all-reduce(f32[]{:T(128)S(6)} %add.278), channel_id=1, replica_groups=mesh['dp'=8,'mp'=4] {'dp','mp'}, use_global_device_ids=true, to_apply=%region_29.30 | all-reduce | flops 1 | bytes 8 | tf_op jit(solution)/shard_map/psum | solution.py:227
  1438.1 10.7 reduce-scatter.11.cloned.1.call-done
  1448.7 4.6 add_convert_fusion.1
  1453.4 69.6 %reduce-scatter.13.cloned.1.call-done = bf16[4096,256]{1,0:T(8,128)(2,1)} async-done(((bf16[4096,1024]{1,0:T(8,128)(2,1)}), bf16[4096,256]{1,0:T(8,128)(2,1)}) %reduce-scatter.13.cloned.1.call-update) | async-done | bytes 2097168 | tf_op jit(solution)/shard_map/reduce_scatter | solution.py:204
  1522.9 5.2 convert_add_fusion.1
  (231 shorter events, 155.4 us)
Async XLA Ops:
  7.2 30.7 %copy-start.24 = (f32[128,256]{1,0:T(8,128)S(1)}, f32[128,256]{1,0:T(8,128)}, u32[]{:S(2)}) copy-start(f32[128,256]{1,0:T(8,128)} %param.36) | copy-start | bytes 393220
  7.2 30.7 %copy-start.26 = (f32[256,128]{1,0:T(8,128)S(1)}, f32[256,128]{1,0:T(8,128)}, u32[]{:S(2)}) copy-start(f32[256,128]{1,0:T(8,128)} %param.40) | copy-start | bytes 393220
  7.2 107.4 %all-gather.7.cloned.1.call-start = ((), (), s32[]{:S(2)}) async-start(), calls=%async_computation.8 | async-start | bytes 1179648 | tf_op jit(solution)/shard_map/all_gather | solution.py:116
  9.0 369.1 %all-gather.15.cloned.1.call-start = ((), (), s32[]{:S(2)}) async-start(), calls=%async_computation.20 | async-start | bytes 41943040 | tf_op jit(solution)/shard_map/all_gather | solution.py:149
  9.0 60.8 %copy-start.1 = (bf16[4096,1024]{1,0:T(8,128)(2,1)S(1)}, bf16[4096,1024]{1,0:T(8,128)(2,1)}, u32[]{:S(2)}) copy-start(bf16[4096,1024]{1,0:T(8,128)(2,1)} %param.30) | copy-start | bytes 25165828
  32.2 40.0 %copy-start.34 = (f32[1,1024]{1,0:T(1,128)}, f32[1,1024]{1,0:T(1,128)S(1)}, u32[]{:S(2)}) copy-start(f32[1,1024]{1,0:T(1,128)S(1)} %get-tuple-element.441) | copy-start | bytes 12292
  37.9 32.0 %copy-start.28 = (f32[4096]{0:T(1024)}, f32[4096]{0:T(1024)S(1)}, u32[]{:S(2)}) copy-start(f32[4096]{0:T(1024)S(1)} %get-tuple-element.438) | copy-start | bytes 49156
  69.9 2.3 copy-start.19
  72.1 3.2 copy-start.2
  164.8 6.5 copy-start.30
  164.8 13.4 copy-start.6
  164.8 13.4 copy-start.12
  164.8 13.4 copy-start.13
  164.8 7.8 copy-start.14
  171.3 1.3 copy-start.7
  178.2 2.0 copy-start.20
  178.2 1.2 copy-start.16
  178.3 261.7 %all-gather.9.cloned.1.call-start = ((), (), s32[]{:S(2)}) async-start(), calls=%async_computation.9 | async-start | bytes 3170304 | tf_op jit(solution)/shard_map/all_gather | solution.py:119
  180.2 303.6 %all-gather.11.cloned.1.call-start = ((), (), s32[]{:S(2)}) async-start(), calls=%async_computation.10 | async-start | bytes 1585152 | tf_op jit(solution)/shard_map/all_gather | solution.py:120
  181.0 502.3 %all-reduce.2.cloned.1.call-start = ((), (), s32[]{:S(2)}) async-start(), calls=%async_computation.12 | async-start | bytes 16777216 | tf_op jit(solution)/shard_map/psum | solution.py:172
  439.9 12.5 copy-start.10
  439.9 12.5 copy-start.40
  506.1 13.0 copy-start.42
  531.7 416.3 %all-gather.13.cloned.1.call-start = ((), (), s32[]{:S(2)}) async-start(), calls=%async_computation.18 | async-start | bytes 1310720 | tf_op jit(solution)/shard_map/all_gather | solution.py:207
  695.2 23.2 %copy-start.15 = (bf16[256,1024]{1,0:T(8,128)(2,1)S(1)}, bf16[256,1024]{1,0:T(8,128)(2,1)}, u32[]{:S(2)}) copy-start(bf16[256,1024]{1,0:T(8,128)(2,1)} %all_gather.30) | copy-start | bytes 1572868
  712.7 5.7 copy-start.5
  732.5 6.5 copy-start.4
  739.1 5.7 copy-start
  767.7 6.5 copy-start.4
  774.2 5.7 copy-start
  802.9 6.5 copy-start.4
  809.4 5.7 copy-start
  838.0 6.5 copy-start.4
  844.6 5.7 copy-start
  870.1 6.3 copy-start.3
  874.3 25.6 %copy-start.9 = (bf16[32,8,4,1024]{3,1,2,0:T(8,128)(2,1)}, bf16[32,8,4,1024]{3,1,2,0:T(8,128)(2,1)S(1)}, u32[]{:S(2)}) copy-start(bf16[32,8,4,1024]{3,1,2,0:T(8,128)(2,1)S(1)} %copy.128) | copy-start | bytes 6291460
  876.4 1.6 copy-start.27
  878.6 1.6 copy-start.11
  881.0 120.0 %reduce-scatter.25.cloned.1.call-start = ((), (), s32[]{:S(2)}) async-start(), calls=%async_computation.21 | async-start | bytes 589824
  881.0 18.9 %slice-start = ((s8[8388608]{0:T(1024)(128)(4,1)}), s8[4194304]{0:T(1024)(128)(4,1)S(1)}, s32[]{:S(2)}) async-start(s8[8388608]{0:T(1024)(128)(4,1)} %bitcast.205), calls=%async_computation.22 | async-start | bytes 8388608
  890.7 9.3 slice-start.1
  890.7 9.3 copy-start.29
  890.7 9.3 copy-start.35
  900.0 18.5 %copy-start.37 = (f32[1024]{0:T(1024)S(1)}, f32[1024]{0:T(1024)}, u32[]{:S(2)}) copy-start(f32[1024]{0:T(1024)} %get-tuple-element.368) | copy-start | bytes 12292
  919.5 139.1 %reduce-scatter.21.cloned.1.call-start = ((), (), s32[]{:S(2)}) async-start(), calls=%async_computation.17 | async-start | bytes 3170304 | tf_op jit(solution)/shard_map/reduce_scatter | solution.py:215
  919.6 11.7 copy-start.8
  931.3 193.6 %reduce-scatter.17.cloned.1.call-start = ((), (), s32[]{:S(2)}) async-start(), calls=%async_computation.15 | async-start | bytes 1179648 | tf_op jit(solution)/shard_map/reduce_scatter | solution.py:213
  940.5 250.0 %reduce-scatter.15.cloned.1.call-start = ((), (), s32[]{:S(2)}) async-start(), calls=%async_computation.14 | async-start | bytes 1179648 | tf_op jit(solution)/shard_map/reduce_scatter | solution.py:212
  948.0 314.2 %reduce-scatter.23.cloned.1.call-start = ((), (), s32[]{:S(2)}) async-start(), calls=%async_computation.19 | async-start | bytes 2359296 | tf_op jit(solution)/shard_map/reduce_scatter | solution.py:211
  950.9 422.9 %reduce-scatter.19.cloned.1.call-start = ((), (), s32[]{:S(2)}) async-start(), calls=%async_computation.16 | async-start | bytes 6340608 | tf_op jit(solution)/shard_map/reduce_scatter | solution.py:214
  971.3 3.1 copy-start.41
  974.4 474.4 %reduce-scatter.11.cloned.1.call-start = ((), (), s32[]{:S(2)}) async-start(), calls=%async_computation.11 | async-start | bytes 10485760 | tf_op jit(solution)/shard_map/reduce_scatter | solution.py:162
  986.2 536.7 %reduce-scatter.13.cloned.1.call-start = ((), (), s32[]{:S(2)}) async-start(), calls=%async_computation.13 | async-start | bytes 10485760 | tf_op jit(solution)/shard_map/reduce_scatter | solution.py:204
  999.4 0.9 copy-start.23
  999.4 1.1 copy-start.31
  999.4 1.2 copy-start.32
  999.4 1.4 copy-start.33
  999.5 428.6 %copy-start.25 = (f32[128,256]{1,0:T(8,128)S(1)}, f32[128,256]{1,0:T(8,128)}, u32[]{:S(2)}) copy-start(f32[128,256]{1,0:T(8,128)} %param.36) | copy-start | bytes 393220
  999.5 432.6 %copy-start.21 = (f32[688,128]{1,0:T(8,128)S(1)}, f32[688,128]{1,0:T(8,128)}, u32[]{:S(2)}) copy-start(f32[688,128]{1,0:T(8,128)} %param.48) | copy-start | bytes 1056772
  999.5 435.0 %copy-start.17 = (f32[2,128,688]{1,2,0:T(8,128)S(1)}, f32[2,128,688]{1,2,0:T(8,128)}, u32[]{:S(2)}) copy-start(f32[2,128,688]{1,2,0:T(8,128)} %param.44) | copy-start | bytes 2113540
  1002.1 416.4 %copy-start.38 = (f32[1,128]{1,0:T(1,128)}, f32[1,128]{1,0:T(1,128)S(1)}, u32[]{:S(2)}) copy-start(f32[1,128]{1,0:T(1,128)S(1)} %copy.124) | copy-start | bytes 1540
  1008.2 410.2 %copy-start.39 = (f32[1,128]{1,0:T(1,128)}, f32[1,128]{1,0:T(1,128)S(1)}, u32[]{:S(2)}) copy-start(f32[1,128]{1,0:T(1,128)S(1)} %psum.22) | copy-start | bytes 1540
  1058.6 373.4 %copy-start.22 = (f32[688,128]{1,0:T(8,128)S(1)}, f32[688,128]{1,0:T(8,128)}, u32[]{:S(2)}) copy-start(f32[688,128]{1,0:T(8,128)} %reduce-scatter.21.cloned.1.call-done) | copy-start | bytes 1056772
  1373.7 60.8 %copy-start.18 = (f32[2,128,688]{1,2,0:T(8,128)S(1)}, f32[2,128,688]{1,2,0:T(8,128)}, u32[]{:S(2)}) copy-start(f32[2,128,688]{1,2,0:T(8,128)} %reduce-scatter.19.cloned.1.call-done) | copy-start | bytes 2113540
  (1 other events, 0.7 us)
Sparse Core Ops, SparseCore 0:
  10.8 46.0 all-gather.6
  178.4 199.6 all-gather.14
  380.7 59.2 all-gather.8
  442.4 41.3 all-gather.10
  531.9 151.3 all-reduce.1
  881.1 16.8 all-gather.12
  919.7 62.0 reduce-scatter.24
  986.3 72.3 reduce-scatter.20
  1062.4 62.4 reduce-scatter.16
  1128.2 62.2 reduce-scatter.14
  1195.0 67.1 reduce-scatter.22
  1266.1 107.5 reduce-scatter.18
  1376.5 72.2 reduce-scatter.10
  1451.2 71.7 reduce-scatter.12
